TPU v7x, 256 devices: a whole 4x4x8 slice. The times are simulated.
256 devices in a mesh: view: 16 (over z, x_hi), row: 4 (over x_lo, core), col: 4 (over y).
Axes of the slice: x: 4 (x_hi: 2, x_lo: 2; x = x_hi * 2 + x_lo), y: 4, z: 8, core: 2. Of those that a mesh axis runs over, the one named last changes fastest.
Arguments:
- residual: bfloat16 [16, 32, 128, 1024], P('view', 'row', 'col'), may hold values from -6 to 6
- window_query: bfloat16 [16, 32, 128, 1024], P('view', 'row', 'col'), may hold values from -56 to 56
- window_pairs: bfloat16 [2, 16, 32, 128, 1024], P(None, 'view', 'row', 'col'), may hold values from -4 to 4
- near_output: bfloat16 [1024, 1024], P('view'), may hold values from -0.1875 to 0.1875
- norm_gain: float32 [1024], replicated, may hold values from 0.1 to 1.9
- cross_input: bfloat16 [1024, 3072], P('view'), may hold values from -0.125 to 0.125
- head_gain: float32 [2, 64], replicated, may hold values from 0.7 to 6
- cross_output: bfloat16 [1024, 1024], P('view'), may hold values from -0.1875 to 0.1875
Outputs:
- block_out: bfloat16 [16, 32, 128, 1024], P('view', 'row', 'col')
All inputs are finite; a program needn't handle non-finite values.
Results may differ from a plain program's by a relative error of at most 0.018.
Values may be sent and summed in bfloat16 or wider, within the bound.
A program may use at most 128 MiB of HBM per device.

v0:
```python
import jax
import jax.numpy as jnp
from jax import lax
from jax.sharding import PartitionSpec as P

HEAD_DIM = 64
WINDOW = 13
RADIUS = 6


def padded(block, sides, width):
    for axis, dim in sides:
        count = lax.axis_size(axis)
        forward = [(i, i + 1) for i in range(count - 1)]
        backward = [(target, source) for source, target in forward]
        low = lax.ppermute(
            lax.slice_in_dim(block, block.shape[dim] - width, None, axis=dim), axis, forward
        )
        high = lax.ppermute(lax.slice_in_dim(block, 0, width, axis=dim), axis, backward)
        block = jnp.concatenate([low, block, high], axis=dim)
    return block


def window_mask(span_count, offset, total):
    queried = offset + jnp.arange(span_count, dtype=jnp.int32)
    keyed = offset - RADIUS + jnp.arange(span_count + 2 * RADIUS, dtype=jnp.int32)
    first_at = jnp.clip(queried - RADIUS, 0, total - WINDOW)
    return (keyed[None, :] >= first_at[:, None]) & (
        keyed[None, :] <= first_at[:, None] + WINDOW - 1
    )


def both_masks(tile_rows, tile_cols, row_start, col_start, row_count, col_count):
    by_row = window_mask(tile_rows, row_start, row_count)
    by_col = window_mask(tile_cols, col_start, col_count)
    joined = by_row[:, None, :, None] & by_col[None, :, None, :]
    return joined.reshape(
        tile_rows * tile_cols, (tile_rows + 2 * RADIUS) * (tile_cols + 2 * RADIUS)
    )


def neighborhood(queries, key_tile, value_tile, allowed):
    token_count = queries.shape[0] * queries.shape[1]
    span_total = key_tile.shape[0] * key_tile.shape[1]
    features = queries.shape[2]
    head_count = features // HEAD_DIM
    query_heads = queries.reshape(token_count, head_count, HEAD_DIM).transpose(1, 0, 2)
    key_heads = key_tile.reshape(span_total, head_count, HEAD_DIM).transpose(1, 0, 2)
    value_heads = value_tile.reshape(span_total, head_count, HEAD_DIM).transpose(1, 0, 2)

    def one_head(pieces):
        query_h, key_h, value_h = pieces
        scores = jnp.dot(query_h, key_h.T, preferred_element_type=jnp.float32) * HEAD_DIM ** (-0.5)
        scores = jnp.where(allowed, scores, -jnp.inf)
        highest = jnp.max(scores, axis=1, keepdims=True)
        exponent = jnp.exp(scores - highest)
        summed = jnp.sum(exponent, axis=1, keepdims=True)
        mixture = jnp.dot(
            exponent.astype(jnp.bfloat16), value_h, preferred_element_type=jnp.float32
        )
        return (mixture / summed).astype(jnp.bfloat16)

    result = lax.map(one_head, (query_heads, key_heads, value_heads))
    return result.transpose(1, 0, 2).reshape(token_count, features)


def rms_scale(values, gain_vec, epsilon):
    meansq = jnp.mean(values * values, axis=-1, keepdims=True)
    return values * lax.rsqrt(meansq + epsilon) * gain_vec


def split_projected(projected, head_gain, features):
    token_count = projected.shape[0]
    head_count = features // HEAD_DIM
    queried = rms_scale(
        projected[:, :features].reshape(token_count, head_count, HEAD_DIM), head_gain[0], 1e-06
    )
    keyed = rms_scale(
        projected[:, features : 2 * features].reshape(token_count, head_count, HEAD_DIM),
        head_gain[1],
        1e-06,
    )
    return (
        queried.astype(jnp.bfloat16).reshape(token_count, features),
        keyed.astype(jnp.bfloat16).reshape(token_count, features),
        projected[:, 2 * features :].astype(jnp.bfloat16),
    )


def across(queries, key_views, value_views):
    view_count, token_count, features = queries.shape
    other_count = key_views.shape[0]
    head_count = features // HEAD_DIM
    queried = queries.reshape(view_count, token_count, head_count, HEAD_DIM)
    keyed = key_views.reshape(other_count, token_count, head_count, HEAD_DIM)
    valued = value_views.reshape(other_count, token_count, head_count, HEAD_DIM)
    scores = jnp.einsum(
        "vnhd,wnhd->nhvw", queried, keyed, preferred_element_type=jnp.float32
    ) * HEAD_DIM ** (-0.5)
    highest = jnp.max(scores, axis=3, keepdims=True)
    exponent = jnp.exp(scores - highest)
    summed = jnp.sum(exponent, axis=3)
    mixture = jnp.einsum(
        "nhvw,wnhd->vnhd", exponent.astype(jnp.bfloat16), valued, preferred_element_type=jnp.float32
    )
    mixture = mixture / jnp.transpose(summed, (2, 0, 1))[..., None]
    return mixture.astype(jnp.bfloat16).reshape(view_count, token_count, features)


def row_folder(left_rows, piece):
    return jnp.dot(left_rows, piece, preferred_element_type=jnp.float32)


def attend_pixels(pieces):
    query_part, pair_part = pieces
    return across(query_part[0, :, 0], pair_part[0, :, 0], pair_part[1, :, 0])


def local(
    residual,
    window_query,
    window_pairs,
    near_output,
    norm_gain,
    cross_input,
    head_gain,
    cross_output,
):
    tile_rows = residual.shape[1]
    tile_cols = residual.shape[2]
    features = residual.shape[3]
    token_count = tile_rows * tile_cols
    groups = lax.axis_size("view")
    group_len = token_count // groups
    nearby = padded(window_pairs, (("row", 2), ("col", 3)), RADIUS)
    row_start = lax.axis_index("row") * tile_rows
    col_start = lax.axis_index("col") * tile_cols
    allowed = both_masks(
        tile_rows,
        tile_cols,
        row_start,
        col_start,
        tile_rows * lax.axis_size("row"),
        tile_cols * lax.axis_size("col"),
    )
    attended = neighborhood(window_query[0], nearby[0, 0], nearby[1, 0], allowed)
    near_term = row_folder(attended, lax.all_gather(near_output, "view", axis=0, tiled=True))
    residue = residual[0].reshape(token_count, features)
    hidden = (residue.astype(jnp.float32) + near_term).astype(jnp.bfloat16)
    normed = rms_scale(hidden.astype(jnp.float32), norm_gain, 1e-05).astype(jnp.bfloat16)
    projected = row_folder(normed, lax.all_gather(cross_input, "view", axis=0, tiled=True))
    queried, keyed, valued = split_projected(projected, head_gain, features)
    query_block = queried.reshape(1, 1, groups, group_len, features)
    pair_block = jnp.stack([keyed, valued]).reshape(2, 1, groups, group_len, features)
    mixture = attend_pixels(
        (
            lax.all_to_all(query_block, "view", split_axis=2, concat_axis=1, tiled=True),
            lax.all_to_all(pair_block, "view", split_axis=2, concat_axis=1, tiled=True),
        )
    )
    returned = lax.all_to_all(mixture, "view", split_axis=0, concat_axis=1, tiled=True)
    crossed = returned[0]
    cross_term = row_folder(crossed, lax.all_gather(cross_output, "view", axis=0, tiled=True))
    block_out = (hidden.astype(jnp.float32) + cross_term).astype(jnp.bfloat16)
    return block_out.reshape(1, tile_rows, tile_cols, features)


def solution(mesh):
    in_specs = (
        P("view", "row", "col", None),
        P("view", "row", "col", None),
        P(None, "view", "row", "col", None),
        P("view", None),
        P(),
        P("view", None),
        P(),
        P("view", None),
    )
    out_specs = P("view", "row", "col", None)
    return jax.shard_map(local, mesh=mesh, in_specs=in_specs, out_specs=out_specs, check_vma=False)
```

profile of v0, /device:TPU:8, one launch (start us, length us, event | category | flops | bytes accessed | tf_op | source)
XLA Modules:
  0.0 355.5 jit_solution(18072664135709869636)
XLA Ops:
  7.3 2.7 fusion.42
  10.0 1.8 collective-permute-start
  14.3 3.3 collective-permute-done.1
  19.1 1.7 pad_maximum_fusion.4
  20.8 3.5 collective-permute-start.2
  24.3 3.3 collective-permute-start.3
  27.6 2.5 reshape_squeeze.19
  30.1 2.5 copy.47
  32.9 3.5 collective-permute-done.3
  36.4 2.9 pad_maximum_fusion
  39.7 2.3 copy.45
  42.0 6.0 %reshape_squeeze.20 = bf16[880,16,64]{2,1,0:T(8,128)(2,1)} reshape(bf16[1,1,20,44,1024]{4,3,2,1,0:T(8,128)(2,1)} %copy.45) | data formatting | bytes 3604480 | tf_op jit(solution)/shard_map/reshape;squeeze | solution.py:48
  48.0 4.8 %copy.48 = bf16[16,880,64]{2,1,0:T(8,128)(2,1)} copy(bf16[16,880,64]{2,0,1:T(8,128)(2,1)} %bitcast.74) | data formatting | bytes 3604480
  52.8 2.3 copy.46
  55.1 5.9 %reshape_squeeze.21 = bf16[880,16,64]{2,1,0:T(8,128)(2,1)} reshape(bf16[1,1,20,44,1024]{4,3,2,1,0:T(8,128)(2,1)} %copy.46) | data formatting | bytes 3604480 | tf_op jit(solution)/shard_map/reshape;squeeze | solution.py:49
  61.0 5.0 %copy.49 = bf16[16,880,64]{2,1,0:T(8,128)(2,1)} copy(bf16[16,880,64]{2,0,1:T(8,128)(2,1)} %bitcast.75) | data formatting | bytes 3604480
  66.0 73.5 %while.11 = (s32[]{:T(128)}, bf16[16,256,64]{1,2,0:T(8,128)(2,1)S(1)}, bf16[16,256,64]{2,1,0:T(8,128)(2,1)}, bf16[16,880,64]{2,1,0:T(8,128)(2,1)}, bf16[16,880,6...) while((s32[]{:T(128)}, ...), condition=%wide.region_3.4_spmd.clone, body=%wide.region_0.3_spmd.clone.sunk | while | flops 59506176 | bytes 4612725 | solution.py:63
  139.6 2.4 fusion.23
  142.1 71.8 %all-gather.6.cloned.1.call-done = bf16[1024,3072]{1,0:T(8,128)(2,1)} async-done(((bf16[64,3072]{1,0:T(8,128)(2,1)}), bf16[1024,3072]{1,0:T(8,128)(2,1)}) %all-gather.6.cloned.1.call-update) | async-done | bytes 6291472 | tf_op jit(solution)/shard_map/all_gather | solution.py:151
  213.8 4.7 %fusion.34 = f32[256,3072]{1,0:T(8,128)S(1)} fusion(bf16[1024,3072]{1,0:T(8,128)(2,1)} %all-gather.6.cloned.1.call-done, bf16[256,1024]{1,0:T(8,128)(2,1)S(1)} %get-tuple-element.108, f32[1024]{0:T(1024)S(1)} %copy-done.10, f32[256]{0:T(256)S(1)} %add_rsqrt_fusion.2), kind=kOutput, calls=%fused_computation.52 | convolution fusion | flops 1611661312 | bytes 9966592 | tf_op jit(solution)/shard_map/dot_general | solution.py:111
  218.5 2.1 slice_multiply_fusion
  222.8 2.3 fusion.33
  225.1 4.6 %all-to-all-start.1 = ((bf16[1,1,16,16,1024]{4,3,1,0,2:T(8,128)(2,1)}), bf16[1,1,16,16,1024]{4,3,1,0,2:T(8,128)(2,1)}, u32[]{:S(2)}, u32[]{:S(2)}) async-start(bf16[1,1,16,16,1024]{4,3,1,0,2:T(8,128)(2,1)} %fusion.33), calls=%async_computation.1 | async-start | bytes 1048576 | tf_op jit(solution)/shard_map/all_to_all | solution.py:157
  229.8 2.1 slice.68
  236.3 11.7 %all-to-all-done.1 = bf16[1,1,16,16,1024]{4,3,1,0,2:T(8,128)(2,1)} async-done(((bf16[1,1,16,16,1024]{4,3,1,0,2:T(8,128)(2,1)}), bf16[1,1,16,16,1024]{4,3,1,0,2:T(8,128)(2,1)}, u32[]{:S(2)}, u32[]{:S(2)}) %all-to-all-start.1) | async-done | bytes 524320 | tf_op jit(solution)/shard_map/all_to_all | solution.py:157
  248.1 3.7 %all-to-all-start = ((bf16[2,1,16,16,1024]{4,3,1,0,2:T(8,128)(2,1)}), bf16[2,1,16,16,1024]{4,3,1,0,2:T(8,128)(2,1)S(1)}, u32[]{:S(2)}, u32[]{:S(2)}) async-start(bf16[2,1,16,16,1024]{4,3,1,0,2:T(8,128)(2,1)} %copy.52), calls=%async_computation | async-start | bytes 2097152 | tf_op jit(solution)/shard_map/all_to_all | solution.py:158
  252.5 2.0 reshape_squeeze.23
  254.5 24.7 %all-to-all-done = bf16[2,1,16,16,1024]{4,3,1,0,2:T(8,128)(2,1)S(1)} async-done(((bf16[2,1,16,16,1024]{4,3,1,0,2:T(8,128)(2,1)}), bf16[2,1,16,16,1024]{4,3,1,0,2:T(8,128)(2,1)S(1)}, u32[]{:S(2)}, u32[]{:S(2)}) %all-to-all-start) | async-done | bytes 1048608 | tf_op jit(solution)/shard_map/all_to_all | solution.py:158
  280.0 1.6 reshape_squeeze.22
  287.6 4.2 %all-to-all-start.2 = ((bf16[16,16,1024]{2,1,0:T(8,128)(2,1)}), bf16[16,16,1024]{2,1,0:T(8,128)(2,1)S(1)}, u32[]{:S(2)}, u32[]{:S(2)}) async-start(bf16[16,16,1024]{2,1,0:T(8,128)(2,1)} %reshape.267), calls=%async_computation.2 | async-start | bytes 1048576 | tf_op jit(solution)/shard_map/all_to_all | solution.py:161
  291.8 54.1 %all-gather.8.cloned.1.call-done = bf16[1024,1024]{1,0:T(8,128)(2,1)} async-done(((bf16[64,1024]{1,0:T(8,128)(2,1)}), bf16[1024,1024]{1,0:T(8,128)(2,1)}) %all-gather.8.cloned.1.call-update) | async-done | bytes 2097168 | tf_op jit(solution)/shard_map/all_gather | solution.py:163
  345.9 3.1 fusion.21
  (168 shorter events, 92.4 us)
Async XLA Ops:
  6.5 6.6 %copy-start = (bf16[2,1,8,32,1024]{4,3,2,1,0:T(8,128)(2,1)S(1)}, bf16[2,1,8,32,1024]{4,3,2,1,0:T(8,128)(2,1)}, u32[]{:S(2)}) copy-start(bf16[2,1,8,32,1024]{4,3,2,1,0:T(8,128)(2,1)} %param.12) | copy-start | bytes 3145732
  6.5 133.0 %all-gather.4.cloned.1.call-start = ((), (), s32[]{:S(2)}) async-start(), calls=%async_computation.3 | async-start | bytes 2228224 | tf_op jit(solution)/shard_map/all_gather | solution.py:147
  7.3 6.5 %copy-start.9 = (f32[2,64]{1,0:T(2,128)S(1)}, f32[2,64]{1,0:T(2,128)}, u32[]{:S(2)}) copy-start(f32[2,64]{1,0:T(2,128)} %param.16) | copy-start | bytes 1540
  7.3 206.5 %all-gather.6.cloned.1.call-start = ((), (), s32[]{:S(2)}) async-start(), calls=%async_computation.4 | async-start | bytes 6684672 | tf_op jit(solution)/shard_map/all_gather | solution.py:151
  10.0 3.8 %collective-permute-start = (bf16[2,1,6,32,1024]{4,3,2,1,0:T(8,128)(2,1)}, bf16[2,1,6,32,1024]{4,3,2,1,0:T(8,128)(2,1)S(1)}, u32[]{:S(2)}, u32[]{:S(2)}) collective-permute-start(bf16[2,1,6,32,1024]{4,3,2,1,0:T(8,128)(2,1)} %get-tuple-element.103), channel_id=1, source_target_pairs={{0,4},{4,8},{8,12},{1,5},{5,9},{9,13},{2,6},{6,10},{10,14},{3,7},{... | collective-permute-start | bytes 2359304 | tf_op jit(solution)/shard_map/ppermute | solution.py:16
  11.8 5.8 %collective-permute-start.1 = (bf16[2,1,6,32,1024]{4,3,2,1,0:T(8,128)(2,1)}, bf16[2,1,6,32,1024]{4,3,2,1,0:T(8,128)(2,1)}, u32[]{:S(2)}, u32[]{:S(2)}) collective-permute-start(bf16[2,1,6,32,1024]{4,3,2,1,0:T(8,128)(2,1)} %get-tuple-element.104), channel_id=1, source_target_pairs={{4,0},{8,4},{12,8},{5,1},{9,5},{13,9},{6,2},{10,6},{14,10},{7,3},{... | collective-permute-start | bytes 2359304 | tf_op jit(solution)/shard_map/ppermute | solution.py:19
  20.8 12.1 %collective-permute-start.2 = (bf16[2,1,20,6,1024]{4,2,3,1,0:T(8,128)(2,1)}, bf16[2,1,20,6,1024]{4,2,3,1,0:T(8,128)(2,1)}, u32[]{:S(2)}, u32[]{:S(2)}) collective-permute-start(bf16[2,1,20,6,1024]{4,2,3,1,0:T(8,128)(2,1)} %get-tuple-element.99), channel_id=1, source_target_pairs={{0,1},{1,2},{2,3},{4,5},{5,6},{6,7},{8,9},{9,10},{10,11},{12,13},{... | collective-permute-start | bytes 1474568 | tf_op jit(solution)/shard_map/ppermute | solution.py:16
  24.3 12.1 %collective-permute-start.3 = (bf16[2,1,20,6,1024]{4,2,3,1,0:T(8,128)(2,1)}, bf16[2,1,20,6,1024]{4,2,3,1,0:T(8,128)(2,1)}, u32[]{:S(2)}, u32[]{:S(2)}) collective-permute-start(bf16[2,1,20,6,1024]{4,2,3,1,0:T(8,128)(2,1)} %get-tuple-element.100), channel_id=1, source_target_pairs={{1,0},{2,1},{3,2},{5,4},{6,5},{7,6},{9,8},{10,9},{11,10},{13,12},{... | collective-permute-start | bytes 1474568 | tf_op jit(solution)/shard_map/ppermute | solution.py:19
  61.0 5.0 %copy-start.8 = (bf16[16,256,64]{1,2,0:T(8,128)(2,1)S(1)}, bf16[16,256,64]{1,2,0:T(8,128)(2,1)}, u32[]{:S(2)}) copy-start(bf16[16,256,64]{1,2,0:T(8,128)(2,1)} %custom-call) | copy-start | bytes 1572868
  66.0 73.6 %copy-start.5 = (bf16[1,8,32,1024]{3,2,1,0:T(8,128)(2,1)S(1)}, bf16[1,8,32,1024]{3,2,1,0:T(8,128)(2,1)}, u32[]{:S(2)}) copy-start(bf16[1,8,32,1024]{3,2,1,0:T(8,128)(2,1)} %param.10) | copy-start | bytes 1572868
  139.5 74.3 %copy-start.10 = (f32[1024]{0:T(1024)S(1)}, f32[1024]{0:T(1024)}, u32[]{:S(2)}) copy-start(f32[1024]{0:T(1024)} %param.14) | copy-start | bytes 12292
  142.0 76.4 %copy-start.6 = (bf16[256,1024]{1,0:T(8,128)(2,1)}, bf16[256,1024]{1,0:T(8,128)(2,1)S(1)}, u32[]{:S(2)}) copy-start(bf16[256,1024]{1,0:T(8,128)(2,1)S(1)} %get-tuple-element.108) | copy-start | bytes 1572868
  218.5 2.6 copy-start.2
  222.8 9.1 %copy-start.1 = (f32[256,1024]{1,0:T(8,128)S(1)}, f32[256,1024]{1,0:T(8,128)}, u32[]{:S(2)}) copy-start(f32[256,1024]{1,0:T(8,128)} %get-tuple-element.96) | copy-start | bytes 3145732
  225.1 22.9 %all-to-all-start.1 = ((bf16[1,1,16,16,1024]{4,3,1,0,2:T(8,128)(2,1)}), bf16[1,1,16,16,1024]{4,3,1,0,2:T(8,128)(2,1)}, u32[]{:S(2)}, u32[]{:S(2)}) async-start(bf16[1,1,16,16,1024]{4,3,1,0,2:T(8,128)(2,1)} %fusion.33), calls=%async_computation.1 | async-start | bytes 1048576 | tf_op jit(solution)/shard_map/all_to_all | solution.py:157
  233.7 1.5 copy-start.3
  248.1 31.2 %all-to-all-start = ((bf16[2,1,16,16,1024]{4,3,1,0,2:T(8,128)(2,1)}), bf16[2,1,16,16,1024]{4,3,1,0,2:T(8,128)(2,1)S(1)}, u32[]{:S(2)}, u32[]{:S(2)}) async-start(bf16[2,1,16,16,1024]{4,3,1,0,2:T(8,128)(2,1)} %copy.52), calls=%async_computation | async-start | bytes 2097152 | tf_op jit(solution)/shard_map/all_to_all | solution.py:158
  251.7 94.2 %all-gather.8.cloned.1.call-start = ((), (), s32[]{:S(2)}) async-start(), calls=%async_computation.5 | async-start | bytes 2228224 | tf_op jit(solution)/shard_map/all_gather | solution.py:163
  283.2 1.2 copy-start.4
  285.8 60.1 %copy-start.7 = (bf16[256,1024]{1,0:T(8,128)(2,1)S(1)}, bf16[256,1024]{1,0:T(8,128)(2,1)}, u32[]{:S(2)}) copy-start(bf16[256,1024]{1,0:T(8,128)(2,1)} %copy-done.6) | copy-start | bytes 1572868
  287.6 58.3 %all-to-all-start.2 = ((bf16[16,16,1024]{2,1,0:T(8,128)(2,1)}), bf16[16,16,1024]{2,1,0:T(8,128)(2,1)S(1)}, u32[]{:S(2)}, u32[]{:S(2)}) async-start(bf16[16,16,1024]{2,1,0:T(8,128)(2,1)} %reshape.267), calls=%async_computation.2 | async-start | bytes 1048576 | tf_op jit(solution)/shard_map/all_to_all | solution.py:161
Sparse Core Ops, SparseCore 0:
  9.9 88.6 all-gather.3
  101.3 112.5 all-gather.5
  255.1 90.7 all-gather.7
where the time goes:
time: 357 us; the launch traced here: 356 us
  waiting for transfers between devices  171 us (48%)
  local copies, waits for them, and re-layouts  72.7 us (20%)
  matrix products  53.9 us (15%)
  starting transfers between devices  22.4 us (6%)
  other arithmetic  21.7 us (6%)
  between operations  13.5 us (4%)
    all_gather x1, waiting for transfers between devices, local(): lax.all_gather(cross_input, 'view', axis=0, tiled=True)  71.8 us
    all_gather x1, waiting for transfers between devices, local(): lax.all_gather(cross_output, 'view', axis=0, tiled=True)  54.1 us
    all_to_all x1, waiting for transfers between devices, local(): lax.all_to_all(pair_block, 'view', split_axis=2, concat_axis=1, tiled=True)  24.7 us
    and x32, local copies, waits for them, and re-layouts, both_masks(): joined = by_row[:, None, :, None] & by_col[None, :, None, :]  22 us
    dot_general x16, matrix products, one_head(): jnp.dot(query_h, key_h.T, preferred_element_type=jnp.float32)  21.1 us
    dot_general x16, matrix products, one_head(): jnp.dot(exponent.astype(jnp.bfloat16), value_h, preferred_element_type=jn...  19.7 us
    unnamed x26, local copies, waits for them, and re-layouts  13.8 us
    all_to_all x1, waiting for transfers between devices, local(): lax.all_to_all(query_block, 'view', split_axis=2, concat_axis=1, tiled=True)  11.7 us
  transfers between devices with their start and end apart: 10, of which 7 were waited for; matrix products, arithmetic and copies ran while one was open for 38% of the time, Pallas kernels for 0%

commit v1 on v0

--- a/solution.py
+++ b/solution.py
@@ -148,7 +148,12 @@
     residue = residual[0].reshape(token_count, features)
     hidden = (residue.astype(jnp.float32) + near_term).astype(jnp.bfloat16)
     normed = rms_scale(hidden.astype(jnp.float32), norm_gain, 1e-05).astype(jnp.bfloat16)
-    projected = row_folder(normed, lax.all_gather(cross_input, "view", axis=0, tiled=True))
+    projected = row_folder(
+        normed,
+        jnp.concatenate(
+            lax.all_to_all(jnp.stack([cross_input] * lax.axis_size("view")), "view", 0, 0), axis=0
+        ),
+    )
     queried, keyed, valued = split_projected(projected, head_gain, features)
     query_block = queried.reshape(1, 1, groups, group_len, features)
     pair_block = jnp.stack([keyed, valued]).reshape(2, 1, groups, group_len, features)

time: 357 us -> 334 us (0.936)
  waiting for transfers between devices: 171 us -> 131 us
  starting transfers between devices: 22.4 us -> 34.4 us
    all_gather x1 -> x0, waiting for transfers between devices: 71.8 us -> none  [local(): lax.all_gather(cross_input, 'view', axis=0, tiled=True)]
    all_gather x1, waiting for transfers between devices: 0.02 us -> 30.1 us  [local(): lax.all_gather(near_output, 'view', axis=0, tiled=True)]
    all_to_all x0 -> x1, starting transfers between devices: none -> 11.2 us  [local(): lax.all_to_all(jnp.stack([cross_input] * lax.axis_size('view')), 'view',...]
    ppermute x2, waiting for transfers between devices: 0.11 us -> 5.53 us  [padded(): lax.ppermute(lax.slice_in_dim(block, block.shape[dim] - width, None, axis...]
    unnamed x26 -> x28, local copies, waits for them, and re-layouts: 13.8 us -> 13.6 us
  transfers between devices with their start and end apart: 10 -> 10, of which waited for: 7 -> 6; matrix products, arithmetic and copies ran while one was open for 38% -> 40% of each run, Pallas kernels for 0% -> 0%
where the time goes in v1:
time: 334 us; the launch traced here: 332 us
  waiting for transfers between devices  131 us (39%)
  local copies, waits for them, and re-layouts  75.9 us (23%)
  matrix products  54.1 us (16%)
  starting transfers between devices  34.4 us (10%)
  other arithmetic  21.6 us (6%)
  between operations  13.8 us (4%)
    all_gather x1, waiting for transfers between devices, local(): lax.all_gather(cross_output, 'view', axis=0, tiled=True)  53.2 us
    all_gather x1, waiting for transfers between devices, local(): lax.all_gather(near_output, 'view', axis=0, tiled=True)  30.1 us
    all_to_all x1, waiting for transfers between devices, local(): lax.all_to_all(pair_block, 'view', split_axis=2, concat_axis=1, tiled=True)  26.3 us
    and x32, local copies, waits for them, and re-layouts, both_masks(): joined = by_row[:, None, :, None] & by_col[None, :, None, :]  22 us
    dot_general x16, matrix products, one_head(): jnp.dot(query_h, key_h.T, preferred_element_type=jnp.float32)  21 us
    dot_general x16, matrix products, one_head(): jnp.dot(exponent.astype(jnp.bfloat16), value_h, preferred_element_type=jn...  19.7 us
    unnamed x28, local copies, waits for them, and re-layouts  13.6 us
    all_to_all x1, waiting for transfers between devices, local(): lax.all_to_all(query_block, 'view', split_axis=2, concat_axis=1, tiled=True)  11.6 us
  transfers between devices with their start and end apart: 10, of which 6 were waited for; matrix products, arithmetic and copies ran while one was open for 40% of the time, Pallas kernels for 0%

profile of v1, /device:TPU:8, one launch (start us, length us, event | category | flops | bytes accessed | tf_op | source)
XLA Modules:
  0.0 331.7 jit_solution(7150141769788678404)
XLA Ops:
  6.5 2.8 fusion.42
  9.3 1.8 collective-permute-start
  12.4 3.4 %stack.6 = bf16[16,64,3072]{2,1,0:T(8,128)(2,1)} broadcast(bf16[64,3072]{1,0:T(8,128)(2,1)S(1)} %copy-done.9), dimensions={1,2} | broadcast | bytes 6684672 | tf_op jit(solution)/shard_map/stack | solution.py:154
  15.8 11.2 %all-to-all-start = ((bf16[16,64,3072]{2,1,0:T(8,128)(2,1)}), bf16[16,64,3072]{2,1,0:T(8,128)(2,1)}, u32[]{:S(2)}, u32[]{:S(2)}) async-start(bf16[16,64,3072]{2,1,0:T(8,128)(2,1)} %stack.6), calls=%async_computation | async-start | bytes 12582912 | tf_op jit(solution)/shard_map/all_to_all | solution.py:154
  31.3 3.5 %collective-permute-start.2 = (bf16[2,1,20,6,1024]{4,2,3,1,0:T(8,128)(2,1)}, bf16[2,1,20,6,1024]{4,2,3,1,0:T(8,128)(2,1)}, u32[]{:S(2)}, u32[]{:S(2)}) collective-permute-start(bf16[2,1,20,6,1024]{4,2,3,1,0:T(8,128)(2,1)} %get-tuple-element.99), channel_id=1, source_target_pairs={{0,1},{1,2},{2,3},{4,5},{5,6},{6,7},{8,9},{9,10},{10,11},{12,13},{... | collective-permute-start | bytes 1474568 | tf_op jit(solution)/shard_map/ppermute | solution.py:16
  34.8 3.3 %collective-permute-start.3 = (bf16[2,1,20,6,1024]{4,2,3,1,0:T(8,128)(2,1)}, bf16[2,1,20,6,1024]{4,2,3,1,0:T(8,128)(2,1)}, u32[]{:S(2)}, u32[]{:S(2)}) collective-permute-start(bf16[2,1,20,6,1024]{4,2,3,1,0:T(8,128)(2,1)} %get-tuple-element.100), channel_id=1, source_target_pairs={{1,0},{2,1},{3,2},{5,4},{6,5},{7,6},{9,8},{10,9},{11,10},{13,12},{... | collective-permute-start | bytes 1474568 | tf_op jit(solution)/shard_map/ppermute | solution.py:19
  38.2 2.5 reshape_squeeze.19
  40.7 2.5 copy.47
  43.4 5.5 %collective-permute-done.2 = bf16[2,1,20,6,1024]{4,2,3,1,0:T(8,128)(2,1)} collective-permute-done((bf16[2,1,20,6,1024]{4,2,3,1,0:T(8,128)(2,1)}, bf16[2,1,20,6,1024]{4,2,3,1,0:T(8,128)(2,1)}, u32[]{:S(2)}, u32[]{:S(2)}) %collective-permute-start.2) | collective-permute-done | bytes 491552 | tf_op jit(solution)/shard_map/ppermute | solution.py:16
  49.0 3.8 %collective-permute-done.3 = bf16[2,1,20,6,1024]{4,2,3,1,0:T(8,128)(2,1)} collective-permute-done((bf16[2,1,20,6,1024]{4,2,3,1,0:T(8,128)(2,1)}, bf16[2,1,20,6,1024]{4,2,3,1,0:T(8,128)(2,1)}, u32[]{:S(2)}, u32[]{:S(2)}) %collective-permute-start.3) | collective-permute-done | bytes 491552 | tf_op jit(solution)/shard_map/ppermute | solution.py:19
  52.8 2.9 pad_maximum_fusion
  56.1 2.3 copy.45
  58.4 5.9 %reshape_squeeze.20 = bf16[880,16,64]{2,1,0:T(8,128)(2,1)} reshape(bf16[1,1,20,44,1024]{4,3,2,1,0:T(8,128)(2,1)} %copy.45) | data formatting | bytes 3604480 | tf_op jit(solution)/shard_map/reshape;squeeze | solution.py:48
  64.3 4.7 %copy.48 = bf16[16,880,64]{2,1,0:T(8,128)(2,1)} copy(bf16[16,880,64]{2,0,1:T(8,128)(2,1)} %bitcast.75) | data formatting | bytes 3604480
  69.1 2.3 copy.46
  71.3 5.9 %reshape_squeeze.21 = bf16[880,16,64]{2,1,0:T(8,128)(2,1)} reshape(bf16[1,1,20,44,1024]{4,3,2,1,0:T(8,128)(2,1)} %copy.46) | data formatting | bytes 3604480 | tf_op jit(solution)/shard_map/reshape;squeeze | solution.py:49
  77.3 4.8 %copy.49 = bf16[16,880,64]{2,1,0:T(8,128)(2,1)} copy(bf16[16,880,64]{2,0,1:T(8,128)(2,1)} %bitcast.76) | data formatting | bytes 3604480
  82.1 73.5 %while.11 = (s32[]{:T(128)}, bf16[16,256,64]{1,2,0:T(8,128)(2,1)S(1)}, bf16[16,256,64]{2,1,0:T(8,128)(2,1)}, bf16[16,880,64]{2,1,0:T(8,128)(2,1)}, bf16[16,880,6...) while((s32[]{:T(128)}, ...), condition=%wide.region_3.4_spmd.clone, body=%wide.region_0.3_spmd.clone.sunk | while | flops 59506176 | bytes 4612725 | solution.py:63
  155.6 30.1 %all-gather.3.cloned.1.call-done = bf16[1024,1024]{1,0:T(8,128)(2,1)} async-done(((bf16[64,1024]{1,0:T(8,128)(2,1)}), bf16[1024,1024]{1,0:T(8,128)(2,1)}) %all-gather.3.cloned.1.call-update) | async-done | bytes 2097168 | tf_op jit(solution)/shard_map/all_gather | solution.py:147
  185.6 2.4 fusion.23
  188.1 4.8 %fusion.34 = f32[256,3072]{1,0:T(8,128)S(1)} fusion(bf16[1024,3072]{1,0:T(8,128)(2,1)} %bitcast.6, bf16[256,1024]{1,0:T(8,128)(2,1)S(1)} %get-tuple-element.108, f32[1024]{0:T(1024)S(1)} %copy-done.11, f32[256]{0:T(256)S(1)} %add_rsqrt_fusion.2), kind=kOutput, calls=%fused_computation.52 | convolution fusion | flops 1611661312 | bytes 9966592 | tf_op jit(solution)/shard_map/dot_general | solution.py:111
  193.0 2.1 slice_multiply_fusion
  197.3 2.3 fusion.33
  199.6 6.0 %all-to-all-start.2 = ((bf16[1,1,16,16,1024]{4,3,1,0,2:T(8,128)(2,1)}), bf16[1,1,16,16,1024]{4,3,1,0,2:T(8,128)(2,1)}, u32[]{:S(2)}, u32[]{:S(2)}) async-start(bf16[1,1,16,16,1024]{4,3,1,0,2:T(8,128)(2,1)} %fusion.33), calls=%async_computation.2 | async-start | bytes 1048576 | tf_op jit(solution)/shard_map/all_to_all | solution.py:162
  205.7 2.1 slice.68
  212.2 11.6 %all-to-all-done.2 = bf16[1,1,16,16,1024]{4,3,1,0,2:T(8,128)(2,1)} async-done(((bf16[1,1,16,16,1024]{4,3,1,0,2:T(8,128)(2,1)}), bf16[1,1,16,16,1024]{4,3,1,0,2:T(8,128)(2,1)}, u32[]{:S(2)}, u32[]{:S(2)}) %all-to-all-start.2) | async-done | bytes 524320 | tf_op jit(solution)/shard_map/all_to_all | solution.py:162
  223.8 3.7 %all-to-all-start.1 = ((bf16[2,1,16,16,1024]{4,3,1,0,2:T(8,128)(2,1)}), bf16[2,1,16,16,1024]{4,3,1,0,2:T(8,128)(2,1)S(1)}, u32[]{:S(2)}, u32[]{:S(2)}) async-start(bf16[2,1,16,16,1024]{4,3,1,0,2:T(8,128)(2,1)} %copy.52), calls=%async_computation.1 | async-start | bytes 2097152 | tf_op jit(solution)/shard_map/all_to_all | solution.py:163
  228.2 2.0 reshape_squeeze.23
  230.3 26.3 %all-to-all-done.1 = bf16[2,1,16,16,1024]{4,3,1,0,2:T(8,128)(2,1)S(1)} async-done(((bf16[2,1,16,16,1024]{4,3,1,0,2:T(8,128)(2,1)}), bf16[2,1,16,16,1024]{4,3,1,0,2:T(8,128)(2,1)S(1)}, u32[]{:S(2)}, u32[]{:S(2)}) %all-to-all-start.1) | async-done | bytes 1048608 | tf_op jit(solution)/shard_map/all_to_all | solution.py:163
  265.0 3.6 %all-to-all-start.3 = ((bf16[16,16,1024]{2,1,0:T(8,128)(2,1)}), bf16[16,16,1024]{2,1,0:T(8,128)(2,1)S(1)}, u32[]{:S(2)}, u32[]{:S(2)}) async-start(bf16[16,16,1024]{2,1,0:T(8,128)(2,1)} %reshape.273), calls=%async_computation.3 | async-start | bytes 1048576 | tf_op jit(solution)/shard_map/all_to_all | solution.py:166
  268.6 53.2 %all-gather.5.cloned.1.call-done = bf16[1024,1024]{1,0:T(8,128)(2,1)} async-done(((bf16[64,1024]{1,0:T(8,128)(2,1)}), bf16[1024,1024]{1,0:T(8,128)(2,1)}) %all-gather.5.cloned.1.call-update) | async-done | bytes 2097168 | tf_op jit(solution)/shard_map/all_gather | solution.py:168
  321.8 3.1 fusion.21
  (170 shorter events, 94.7 us)
Async XLA Ops:
  6.5 5.9 %copy-start.9 = (bf16[64,3072]{1,0:T(8,128)(2,1)S(1)}, bf16[64,3072]{1,0:T(8,128)(2,1)}, u32[]{:S(2)}) copy-start(bf16[64,3072]{1,0:T(8,128)(2,1)} %param.15) | copy-start | bytes 1179652
  6.5 179.1 %all-gather.3.cloned.1.call-start = ((), (), s32[]{:S(2)}) async-start(), calls=%async_computation.4 | async-start | bytes 2228224 | tf_op jit(solution)/shard_map/all_gather | solution.py:147
  9.3 18.4 %collective-permute-start = (bf16[2,1,6,32,1024]{4,3,2,1,0:T(8,128)(2,1)}, bf16[2,1,6,32,1024]{4,3,2,1,0:T(8,128)(2,1)S(1)}, u32[]{:S(2)}, u32[]{:S(2)}) collective-permute-start(bf16[2,1,6,32,1024]{4,3,2,1,0:T(8,128)(2,1)} %get-tuple-element.103), channel_id=1, source_target_pairs={{0,4},{4,8},{8,12},{1,5},{5,9},{9,13},{2,6},{6,10},{10,14},{3,7},{... | collective-permute-start | bytes 2359304 | tf_op jit(solution)/shard_map/ppermute | solution.py:16
  11.1 17.1 %collective-permute-start.1 = (bf16[2,1,6,32,1024]{4,3,2,1,0:T(8,128)(2,1)}, bf16[2,1,6,32,1024]{4,3,2,1,0:T(8,128)(2,1)}, u32[]{:S(2)}, u32[]{:S(2)}) collective-permute-start(bf16[2,1,6,32,1024]{4,3,2,1,0:T(8,128)(2,1)} %get-tuple-element.104), channel_id=1, source_target_pairs={{4,0},{8,4},{12,8},{5,1},{9,5},{13,9},{6,2},{10,6},{14,10},{7,3},{... | collective-permute-start | bytes 2359304 | tf_op jit(solution)/shard_map/ppermute | solution.py:19
  15.8 11.2 %copy-start = (bf16[2,1,8,32,1024]{4,3,2,1,0:T(8,128)(2,1)S(1)}, bf16[2,1,8,32,1024]{4,3,2,1,0:T(8,128)(2,1)}, u32[]{:S(2)}) copy-start(bf16[2,1,8,32,1024]{4,3,2,1,0:T(8,128)(2,1)} %param.12) | copy-start | bytes 3145732
  15.8 172.3 %all-to-all-start = ((bf16[16,64,3072]{2,1,0:T(8,128)(2,1)}), bf16[16,64,3072]{2,1,0:T(8,128)(2,1)}, u32[]{:S(2)}, u32[]{:S(2)}) async-start(bf16[16,64,3072]{2,1,0:T(8,128)(2,1)} %stack.6), calls=%async_computation | async-start | bytes 12582912 | tf_op jit(solution)/shard_map/all_to_all | solution.py:154
  27.1 0.7 copy-start.10
  31.3 17.6 %collective-permute-start.2 = (bf16[2,1,20,6,1024]{4,2,3,1,0:T(8,128)(2,1)}, bf16[2,1,20,6,1024]{4,2,3,1,0:T(8,128)(2,1)}, u32[]{:S(2)}, u32[]{:S(2)}) collective-permute-start(bf16[2,1,20,6,1024]{4,2,3,1,0:T(8,128)(2,1)} %get-tuple-element.99), channel_id=1, source_target_pairs={{0,1},{1,2},{2,3},{4,5},{5,6},{6,7},{8,9},{9,10},{10,11},{12,13},{... | collective-permute-start | bytes 1474568 | tf_op jit(solution)/shard_map/ppermute | solution.py:16
  34.8 17.9 %collective-permute-start.3 = (bf16[2,1,20,6,1024]{4,2,3,1,0:T(8,128)(2,1)}, bf16[2,1,20,6,1024]{4,2,3,1,0:T(8,128)(2,1)}, u32[]{:S(2)}, u32[]{:S(2)}) collective-permute-start(bf16[2,1,20,6,1024]{4,2,3,1,0:T(8,128)(2,1)} %get-tuple-element.100), channel_id=1, source_target_pairs={{1,0},{2,1},{3,2},{5,4},{6,5},{7,6},{9,8},{10,9},{11,10},{13,12},{... | collective-permute-start | bytes 1474568 | tf_op jit(solution)/shard_map/ppermute | solution.py:19
  77.3 4.8 %copy-start.8 = (bf16[16,256,64]{1,2,0:T(8,128)(2,1)S(1)}, bf16[16,256,64]{1,2,0:T(8,128)(2,1)}, u32[]{:S(2)}) copy-start(bf16[16,256,64]{1,2,0:T(8,128)(2,1)} %custom-call) | copy-start | bytes 1572868
  82.1 103.6 %copy-start.5 = (bf16[1,8,32,1024]{3,2,1,0:T(8,128)(2,1)S(1)}, bf16[1,8,32,1024]{3,2,1,0:T(8,128)(2,1)}, u32[]{:S(2)}) copy-start(bf16[1,8,32,1024]{3,2,1,0:T(8,128)(2,1)} %param.10) | copy-start | bytes 1572868
  155.6 32.5 %copy-start.11 = (f32[1024]{0:T(1024)S(1)}, f32[1024]{0:T(1024)}, u32[]{:S(2)}) copy-start(f32[1024]{0:T(1024)} %param.14) | copy-start | bytes 12292
  188.1 4.9 %copy-start.6 = (bf16[256,1024]{1,0:T(8,128)(2,1)}, bf16[256,1024]{1,0:T(8,128)(2,1)S(1)}, u32[]{:S(2)}) copy-start(bf16[256,1024]{1,0:T(8,128)(2,1)S(1)} %get-tuple-element.108) | copy-start | bytes 1572868
  193.0 2.6 copy-start.2
  197.3 10.5 %copy-start.1 = (f32[256,1024]{1,0:T(8,128)S(1)}, f32[256,1024]{1,0:T(8,128)}, u32[]{:S(2)}) copy-start(f32[256,1024]{1,0:T(8,128)} %get-tuple-element.96) | copy-start | bytes 3145732
  199.6 24.2 %all-to-all-start.2 = ((bf16[1,1,16,16,1024]{4,3,1,0,2:T(8,128)(2,1)}), bf16[1,1,16,16,1024]{4,3,1,0,2:T(8,128)(2,1)}, u32[]{:S(2)}, u32[]{:S(2)}) async-start(bf16[1,1,16,16,1024]{4,3,1,0,2:T(8,128)(2,1)} %fusion.33), calls=%async_computation.2 | async-start | bytes 1048576 | tf_op jit(solution)/shard_map/all_to_all | solution.py:162
  209.6 1.5 copy-start.3
  223.8 32.7 %all-to-all-start.1 = ((bf16[2,1,16,16,1024]{4,3,1,0,2:T(8,128)(2,1)}), bf16[2,1,16,16,1024]{4,3,1,0,2:T(8,128)(2,1)S(1)}, u32[]{:S(2)}, u32[]{:S(2)}) async-start(bf16[2,1,16,16,1024]{4,3,1,0,2:T(8,128)(2,1)} %copy.52), calls=%async_computation.1 | async-start | bytes 2097152 | tf_op jit(solution)/shard_map/all_to_all | solution.py:163
  227.5 94.2 %all-gather.5.cloned.1.call-start = ((), (), s32[]{:S(2)}) async-start(), calls=%async_computation.5 | async-start | bytes 2228224 | tf_op jit(solution)/shard_map/all_gather | solution.py:168
  260.5 1.2 copy-start.4
  263.2 58.6 %copy-start.7 = (bf16[256,1024]{1,0:T(8,128)(2,1)S(1)}, bf16[256,1024]{1,0:T(8,128)(2,1)}, u32[]{:S(2)}) copy-start(bf16[256,1024]{1,0:T(8,128)(2,1)} %copy-done.6) | copy-start | bytes 1572868
  265.0 56.8 %all-to-all-start.3 = ((bf16[16,16,1024]{2,1,0:T(8,128)(2,1)}), bf16[16,16,1024]{2,1,0:T(8,128)(2,1)S(1)}, u32[]{:S(2)}, u32[]{:S(2)}) async-start(bf16[16,16,1024]{2,1,0:T(8,128)(2,1)} %reshape.273), calls=%async_computation.3 | async-start | bytes 1048576 | tf_op jit(solution)/shard_map/all_to_all | solution.py:166
Sparse Core Ops, SparseCore 0:
  12.6 173.0 all-gather.2
  230.9 90.7 all-gather.4
